TPU v7x, 32 devices: a whole 2x2x4 slice. The times are simulated.
32 devices in a mesh: dp: 8 (over y, x, core), tensor: 4 (over z).
Axes of the slice: x: 2, y: 2, z: 4, core: 2. Of those that a mesh axis runs over, the one named last changes fastest.
Arguments:
- short_tokens: bfloat16 [16, 256, 768], P('dp'), may hold values from -6 to 6
- short_lengths: int32 [16], P('dp'), may hold values from 64 to 256, as said below
- long_tokens: bfloat16 [24, 512, 768], P('dp'), may hold values from -6 to 6
- long_lengths: int32 [24], P('dp'), may hold values from 257 to 512, as said below
- w_qkv: bfloat16 [3, 768, 768], P(None, None, 'tensor'), may hold values from -0.21875 to 0.21875
- b_qv: bfloat16 [2, 12, 64], P(None, 'tensor'), may hold values from -3 to 3
- w_out: bfloat16 [768, 768], P('tensor'), may hold values from -2.5 to 2.5
- res_biases: bfloat16 [2, 768], replicated, may hold values from -3 to 3
- ln_gains: bfloat16 [2, 768], replicated, may hold values from 0.099609375 to 1.8984375
- ln_shifts: bfloat16 [2, 768], replicated, may hold values from -3 to 3
- w_up: bfloat16 [768, 3072], P(None, 'tensor'), may hold values from -0.21875 to 0.21875
- b_up: bfloat16 [4, 768], P('tensor'), may hold values from -3 to 3
- w_down: bfloat16 [3072, 768], P('tensor'), may hold values from -0.109375 to 0.109375
- short_cotangent: bfloat16 [16, 256, 768], P('dp'), may hold values from -6 to 6
- long_cotangent: bfloat16 [24, 512, 768], P('dp'), may hold values from -6 to 6
Outputs:
- short_encoded: bfloat16 [16, 256, 768], P('dp')
- long_encoded: bfloat16 [24, 512, 768], P('dp')
- short_grad_tokens: float32 [16, 256, 768], P('dp')
- long_grad_tokens: float32 [24, 512, 768], P('dp')
- grad_qkv: float32 [3, 768, 768], P(None, 'dp', 'tensor')
- grad_qv_bias: float32 [2, 12, 64], P(None, 'tensor', 'dp')
- grad_out: float32 [768, 768], P('tensor', 'dp')
- grad_res_biases: float32 [2, 768], P(None, 'dp')
- grad_gains: float32 [2, 768], P(None, 'dp')
- grad_shifts: float32 [2, 768], P(None, 'dp')
- grad_up: float32 [768, 3072], P('dp', 'tensor')
- grad_up_bias: float32 [4, 768], P('tensor', 'dp')
- grad_down: float32 [3072, 768], P('tensor', 'dp')
Inputs may be any that keep to these rules, and one draw needn't show every extreme that they name: `short_lengths`: the first short pair has 256 valid tokens. `long_lengths`: the first long pair has 512 valid tokens.
All inputs are finite; a program needn't handle non-finite values.
Results may differ from a plain program's by a relative error of at most 0.013.
The roundings to bfloat16 on the way count: a program that leaves them out, or rounds other values in their place, can miss the bound.
Values sent between devices are 32-bit elements; how exact they have to be, the bound alone decides.
No kernel may reach another device: no remote copies, remote signals or barrier semaphores. Data moves between devices by JAX's collectives and lax.ppermute only.
A program may use at most 128 MiB of HBM per device.

v0:
```python
import jax
import jax.numpy as jnp
from jax import lax
from jax.sharding import PartitionSpec as P

HD = 64
EPSILON = 1e-12


def normalize(hidden):
    center = hidden - jnp.mean(hidden, -1, keepdims=True)
    factor = lax.rsqrt(jnp.mean(center * center, -1, keepdims=True) + EPSILON)
    return (center * factor, factor[:, 0])


def norm_back(upstream, normed, factor, gain):
    scaled = upstream * gain
    inner_mean = jnp.mean(scaled, -1, keepdims=True)
    cross_mean = jnp.mean(scaled * normed, -1, keepdims=True)
    return factor[:, None] * (scaled - inner_mean - normed * cross_mean)


def gelu_exact(inner):
    return jax.nn.gelu(inner, approximate=False)


def masked_scores(queries, key_rows, length):
    scores = jnp.einsum(
        "qhe,khe->hqk", queries, key_rows, preferred_element_type=jnp.float32
    ) * HD ** (-0.5)
    visible = jnp.arange(key_rows.shape[0]) < length
    return jnp.where(visible[None, None, :], scores, -1e30)


def attend(queries, key_rows, value_rows, length):
    scores = masked_scores(queries, key_rows, length)
    largest = jnp.max(scores, -1, keepdims=True)
    weights_exp = jnp.exp(scores - largest)
    total = jnp.sum(weights_exp, -1, keepdims=True)
    probs = weights_exp / total
    mixed = jnp.einsum(
        "hqk,khe->qhe", probs.astype(jnp.bfloat16), value_rows, preferred_element_type=jnp.float32
    )
    log_total = largest[..., 0] + jnp.log(total[..., 0])
    return (mixed.astype(jnp.bfloat16), log_total)


def attend_back(queries, key_rows, value_rows, length, log_total, grad_mixed):
    scores = masked_scores(queries, key_rows, length)
    probs = jnp.exp(scores - log_total[..., None])
    grad_values = jnp.einsum(
        "hqk,qhe->khe", probs.astype(jnp.bfloat16), grad_mixed, preferred_element_type=jnp.float32
    )
    grad_probs = jnp.einsum(
        "qhe,khe->hqk", grad_mixed, value_rows, preferred_element_type=jnp.float32
    )
    centered = jnp.sum(probs * grad_probs, -1, keepdims=True)
    grad_scores = (probs * (grad_probs - centered)).astype(jnp.bfloat16)
    grad_queries = jnp.einsum(
        "hqk,khe->qhe", grad_scores, key_rows, preferred_element_type=jnp.float32
    ) * HD ** (-0.5)
    grad_keys = jnp.einsum(
        "hqk,qhe->khe", grad_scores, queries, preferred_element_type=jnp.float32
    ) * HD ** (-0.5)
    return (grad_queries, grad_keys, grad_values)


def forward_pair(item_tuple):
    pair_q, pair_k, pair_v, length = item_tuple
    return attend(pair_q, pair_k, pair_v, length)


def backward_pair(item_tuple):
    pair_q, pair_k, pair_v, length, pair_lse, pair_grad = item_tuple
    return attend_back(pair_q, pair_k, pair_v, length, pair_lse, pair_grad)


def on_device(
    short_tokens,
    short_lengths,
    long_tokens,
    long_lengths,
    w_qkv,
    b_qv,
    w_out,
    res_biases,
    ln_gains,
    ln_shifts,
    w_up,
    b_up,
    w_down,
    short_cotangent,
    long_cotangent,
):
    short_pairs, short_slot, model_width = short_tokens.shape
    long_pairs, long_slot = (long_tokens.shape[0], long_tokens.shape[1])
    short_rows = short_pairs * short_slot
    long_rows = long_pairs * long_slot
    local_width = w_qkv.shape[2]
    heads_here = b_qv.shape[1]
    head_size = b_qv.shape[2]
    flat = jnp.concatenate(
        [
            short_tokens.reshape(short_rows, model_width),
            long_tokens.reshape(long_rows, model_width),
        ],
        0,
    )
    flat_float = flat.astype(jnp.float32)
    gain_rows = ln_gains.astype(jnp.float32)
    shift_rows = ln_shifts.astype(jnp.float32)
    bias_float = res_biases.astype(jnp.float32)
    projected = jnp.einsum("rd,cde->cre", flat, w_qkv, preferred_element_type=jnp.float32)
    bias_rows = jnp.stack(
        [
            b_qv[0].reshape(local_width).astype(jnp.float32),
            jnp.zeros((local_width,), jnp.float32),
            b_qv[1].reshape(local_width).astype(jnp.float32),
        ]
    )
    projected = (projected + bias_rows[:, None, :]).astype(jnp.bfloat16)
    short_proj = projected[:, :short_rows].reshape(
        3, short_pairs, short_slot, heads_here, head_size
    )
    long_proj = projected[:, short_rows:].reshape(3, long_pairs, long_slot, heads_here, head_size)
    short_att, short_lse = lax.map(
        forward_pair, (short_proj[0], short_proj[1], short_proj[2], short_lengths)
    )
    long_att, long_lse = lax.map(
        forward_pair, (long_proj[0], long_proj[1], long_proj[2], long_lengths)
    )
    mixed = jnp.concatenate(
        [short_att.reshape(short_rows, local_width), long_att.reshape(long_rows, local_width)], 0
    )
    attn_part = jnp.dot(mixed, w_out, preferred_element_type=jnp.float32)
    attn_total = lax.psum(attn_part, "tensor")
    normed_one, factor_one = normalize(flat_float + attn_total + bias_float[0])
    first_out = normed_one * gain_rows[0] + shift_rows[0]
    first_low = first_out.astype(jnp.bfloat16)
    inner = jnp.dot(first_low, w_up, preferred_element_type=jnp.float32) + b_up[0].astype(
        jnp.float32
    )
    activated = gelu_exact(inner).astype(jnp.bfloat16)
    ffn_part = jnp.dot(activated, w_down, preferred_element_type=jnp.float32)
    ffn_total = lax.psum(ffn_part, "tensor")
    normed_two, factor_two = normalize(first_out + ffn_total + bias_float[1])
    encoded = (normed_two * gain_rows[1] + shift_rows[1]).astype(jnp.bfloat16)
    upstream = jnp.concatenate(
        [
            short_cotangent.reshape(short_rows, model_width),
            long_cotangent.reshape(long_rows, model_width),
        ],
        0,
    ).astype(jnp.float32)
    grad_second = norm_back(upstream, normed_two, factor_two, gain_rows[1])
    small_second = jnp.stack(
        [jnp.sum(grad_second, 0), jnp.sum(upstream * normed_two, 0), jnp.sum(upstream, 0)]
    )
    grad_branch = grad_second.astype(jnp.bfloat16)
    grad_down = jnp.einsum("rf,rd->fd", activated, grad_branch, preferred_element_type=jnp.float32)
    grad_activated = jnp.einsum(
        "rd,fd->rf", grad_branch, w_down, preferred_element_type=jnp.float32
    )
    ignored_value, gelu_pullback = jax.vjp(gelu_exact, inner)
    grad_inner = gelu_pullback(grad_activated)[0].astype(jnp.bfloat16)
    grad_up = jnp.einsum("rd,rf->df", first_low, grad_inner, preferred_element_type=jnp.float32)
    grad_up_bias = jnp.sum(grad_inner.astype(jnp.float32), 0)[None, :]
    input_part = jnp.einsum("rf,df->rd", grad_inner, w_up, preferred_element_type=jnp.float32)
    up_shard, down_shard, up_bias_shard, small_second_shard = (
        lax.psum_scatter(grad_up, "dp", scatter_dimension=0, tiled=True),
        lax.psum_scatter(grad_down, "dp", scatter_dimension=1, tiled=True),
        lax.psum_scatter(grad_up_bias, "dp", scatter_dimension=1, tiled=True),
        lax.psum_scatter(small_second, "dp", scatter_dimension=1, tiled=True),
    )
    grad_first_out = grad_second + lax.psum(input_part, "tensor")
    grad_first = norm_back(grad_first_out, normed_one, factor_one, gain_rows[0])
    small_first = jnp.stack(
        [
            jnp.sum(grad_first, 0),
            jnp.sum(grad_first_out * normed_one, 0),
            jnp.sum(grad_first_out, 0),
        ]
    )
    grad_attn = grad_first.astype(jnp.bfloat16)
    grad_out = jnp.einsum("rl,rd->ld", mixed, grad_attn, preferred_element_type=jnp.float32)
    grad_mixed = jnp.einsum(
        "rd,ld->rl", grad_attn, w_out, preferred_element_type=jnp.float32
    ).astype(jnp.bfloat16)
    short_grad_mixed = grad_mixed[:short_rows].reshape(
        short_pairs, short_slot, heads_here, head_size
    )
    long_grad_mixed = grad_mixed[short_rows:].reshape(long_pairs, long_slot, heads_here, head_size)
    short_gq, short_gk, short_gv = lax.map(
        backward_pair,
        (short_proj[0], short_proj[1], short_proj[2], short_lengths, short_lse, short_grad_mixed),
    )
    long_gq, long_gk, long_gv = lax.map(
        backward_pair,
        (long_proj[0], long_proj[1], long_proj[2], long_lengths, long_lse, long_grad_mixed),
    )
    short_grads = (
        jnp.stack([short_gq, short_gk, short_gv])
        .astype(jnp.bfloat16)
        .reshape(3, short_rows, local_width)
    )
    long_grads = (
        jnp.stack([long_gq, long_gk, long_gv])
        .astype(jnp.bfloat16)
        .reshape(3, long_rows, local_width)
    )
    grad_projected = jnp.concatenate([short_grads, long_grads], 1)
    grad_qkv = jnp.einsum("rd,cre->cde", flat, grad_projected, preferred_element_type=jnp.float32)
    grad_bias_rows = jnp.sum(grad_projected.astype(jnp.float32), 1)
    grad_qv_bias = jnp.stack([grad_bias_rows[0], grad_bias_rows[2]]).reshape(
        2, heads_here, head_size
    )
    token_part = jnp.einsum(
        "cre,cde->rd", grad_projected, w_qkv, preferred_element_type=jnp.float32
    )
    qkv_shard, qv_bias_shard, out_shard, small_first_shard = (
        lax.psum_scatter(grad_qkv, "dp", scatter_dimension=1, tiled=True),
        lax.psum_scatter(grad_qv_bias, "dp", scatter_dimension=2, tiled=True),
        lax.psum_scatter(grad_out, "dp", scatter_dimension=1, tiled=True),
        lax.psum_scatter(small_first, "dp", scatter_dimension=1, tiled=True),
    )
    grad_tokens = grad_first + lax.psum(token_part, "tensor")
    grad_res_biases = jnp.concatenate([small_first_shard[0:1], small_second_shard[0:1]], 0)
    grad_gains = jnp.concatenate([small_first_shard[1:2], small_second_shard[1:2]], 0)
    grad_shifts = jnp.concatenate([small_first_shard[2:3], small_second_shard[2:3]], 0)
    return (
        encoded[:short_rows].reshape(short_pairs, short_slot, model_width),
        encoded[short_rows:].reshape(long_pairs, long_slot, model_width),
        grad_tokens[:short_rows].reshape(short_pairs, short_slot, model_width),
        grad_tokens[short_rows:].reshape(long_pairs, long_slot, model_width),
        qkv_shard,
        qv_bias_shard,
        out_shard,
        grad_res_biases,
        grad_gains,
        grad_shifts,
        up_shard,
        up_bias_shard,
        down_shard,
    )


def solution(mesh):
    return jax.shard_map(
        on_device,
        mesh=mesh,
        in_specs=(
            P("dp", None, None),
            P("dp"),
            P("dp", None, None),
            P("dp"),
            P(None, None, "tensor"),
            P(None, "tensor", None),
            P("tensor", None),
            P(),
            P(),
            P(),
            P(None, "tensor"),
            P("tensor", None),
            P("tensor", None),
            P("dp", None, None),
            P("dp", None, None),
        ),
        out_specs=(
            P("dp", None, None),
            P("dp", None, None),
            P("dp", None, None),
            P("dp", None, None),
            P(None, "dp", "tensor"),
            P(None, "tensor", "dp"),
            P("tensor", "dp"),
            P(None, "dp"),
            P(None, "dp"),
            P(None, "dp"),
            P("dp", "tensor"),
            P("tensor", "dp"),
            P("tensor", "dp"),
        ),
        check_vma=False,
    )
```

profile of v0, /device:TPU:0, one launch (start us, length us, event | category | flops | bytes accessed | tf_op | source)
XLA Modules:
  0.0 1305.4 jit_solution(6530653363544916583)
XLA Ops:
  21.0 15.0 %while.53 = (s32[]{:T(128)}, bf16[3,512,3,64]{1,3,2,0:T(8,128)(2,1)}, f32[3,3,512]{2,1,0:T(4,128)}, bf16[3,512,3,64]{1,3,2,0:T(8,128)(2,1)S(1)}, s32[3]{0:T(128)...) while((s32[]{:T(128)}, bf16[3,512,3,64]{1,3,2,0:T(8,128)(2,1)}, ...), condition=%wide.region_7.8_spmd, body=%wide.region_4.7_spmd.sunk | while | flops 210861056 | bytes 10283621 | solution.py:129
  43.2 5.3 while.52
  50.9 4.7 fusion.137
  58.1 223.2 %all-reduce.6.cloned.1.call-done = f32[2048,768]{1,0:T(8,128)} async-done(((f32[2048,768]{1,0:T(8,128)}), f32[2048,768]{1,0:T(8,128)}) %all-reduce.6.cloned.1.call-update) | async-done | bytes 6291472 | tf_op jit(solution)/shard_map/psum | solution.py:136
  281.3 4.2 fusion.130
  288.2 18.4 %multiply_convert_fusion.2 = (bf16[2048,768]{1,0:T(8,128)(2,1)S(1)}, f32[2048,768]{1,0:T(8,128)}, f32[2048,768]{1,0:T(8,128)}) fusion(f32[768]{0:T(1024)S(1)} %copy-done.32, bf16[2048,768]{1,0:T(8,128)(2,1)S(1)} %fusion.103, bf16[768,768]{1,0:T(8,128)(2,1)S(1)} %copy-done), kind=kOutput, calls=%fused_computation.132 | convolution fusion | flops 2519728128 | bytes 20057088 | tf_op jit(solution)/shard_map/dot_general | solution.py:140
  308.3 4.6 fusion.138
  313.1 221.7 %all-reduce.8.cloned.1.call-done = f32[2048,768]{1,0:T(8,128)} async-done(((f32[2048,768]{1,0:T(8,128)}), f32[2048,768]{1,0:T(8,128)}) %all-reduce.8.cloned.1.call-update) | async-done | bytes 6291472 | tf_op jit(solution)/shard_map/psum | solution.py:145
  534.8 5.7 fusion.128
  542.4 4.6 fusion.97
  547.0 5.8 fusion.126
  552.9 9.5 convert_reduce_fusion.1
  564.2 4.5 fusion.139
  571.6 219.0 %all-reduce.10.cloned.1.call-done = f32[2048,768]{1,0:T(8,128)} async-done(((f32[2048,768]{1,0:T(8,128)}), f32[2048,768]{1,0:T(8,128)}) %all-reduce.10.cloned.1.call-update) | async-done | bytes 6291472 | tf_op jit(solution)/shard_map/psum | solution.py:175
  790.6 8.1 multiply_reduce_fusion.2
  798.8 4.7 fusion.125
  811.8 25.9 %while.55 = (s32[]{:T(128)}, bf16[3,512,3,64]{1,3,2,0:T(8,128)(2,1)}, bf16[3,512,3,64]{1,3,2,0:T(8,128)(2,1)}, bf16[3,512,3,64]{1,3,2,0:T(8,128)(2,1)}, bf16[3,5...) while((s32[]{:T(128)}, ...), condition=%wide.region_24.25_spmd, body=%wide.region_22.24_spmd.sunk | while | flops 510589952 | bytes 35625200 | solution.py:197
  838.7 5.1 fusion.119
  844.2 9.6 while.54
  866.3 5.1 fusion.116
  871.4 4.3 copy.129
  875.7 4.7 reshape.242
  880.5 6.0 convolution_bitcast_fusion.1
  886.5 7.9 fusion.110
  894.8 7.0 fusion.140
  912.1 13.6 %all-reduce = f32[2,3,64]{2,1,0:T(4,128)S(1)} all-reduce(f32[2,3,64]{2,1,0:T(4,128)S(1)} %reshape.234), channel_id=3, replica_groups=mesh['dp'=8,'tensor'=4] {'dp'}, use_global_device_ids=true, to_apply=%region_28.29.clone | all-reduce | flops 384 | bytes 3072
  929.4 8.8 reduce-scatter.25.cloned.1.call-done
  939.8 42.0 %reduce-scatter.23.cloned.1.call-done = f32[96,576]{1,0:T(8,128)} async-done(((f32[768,576]{1,0:T(8,128)}), f32[96,576]{1,0:T(8,128)}) %reduce-scatter.23.cloned.1.call-update) | async-done | bytes 221200
  983.6 223.4 %all-reduce.12.cloned.1.call-done = f32[2048,768]{1,0:T(8,128)} async-done(((f32[2048,768]{1,0:T(8,128)}), f32[2048,768]{1,0:T(8,128)}) %all-reduce.12.cloned.1.call-update) | async-done | bytes 6291472 | tf_op jit(solution)/shard_map/psum | solution.py:226
  1207.0 5.5 add.175
  1216.2 35.8 %reduce-scatter.21.cloned.1.call-done = f32[768,96]{0,1:T(8,128)} async-done(((f32[768,768]{0,1:T(8,128)}), f32[768,96]{0,1:T(8,128)}) %reduce-scatter.21.cloned.1.call-update) | async-done | bytes 294928 | tf_op jit(solution)/shard_map/reduce_scatter | solution.py:171
  1252.0 46.3 %reduce-scatter.19.cloned.1.call-done = f32[96,768]{1,0:T(8,128)} async-done(((f32[768,768]{1,0:T(8,128)}), f32[96,768]{1,0:T(8,128)}) %reduce-scatter.19.cloned.1.call-update) | async-done | bytes 294928 | tf_op jit(solution)/shard_map/reduce_scatter | solution.py:170
  (326 shorter events, 135.1 us)
Async XLA Ops:
  7.2 281.0 %copy-start = (bf16[768,768]{1,0:T(8,128)(2,1)S(1)}, bf16[768,768]{1,0:T(8,128)(2,1)}, u32[]{:S(2)}) copy-start(bf16[768,768]{1,0:T(8,128)(2,1)} %param.33) | copy-start | bytes 3538948
  7.2 274.1 %all-reduce.6.cloned.1.call-start = ((), (), s32[]{:S(2)}) async-start(), calls=%async_computation.7 | async-start | bytes 12582912 | tf_op jit(solution)/shard_map/psum | solution.py:136
  12.8 8.1 copy-start.40
  21.0 20.5 %copy-start.16 = (bf16[1,512,192]{1,2,0:T(8,128)(2,1)S(1)}, bf16[1,512,192]{1,2,0:T(8,128)(2,1)}, u32[]{:S(2)}) copy-start(bf16[1,512,192]{1,2,0:T(8,128)(2,1)} %get-tuple-element.455) | copy-start | bytes 589828
  21.0 22.1 %copy-start.42 = (s32[2]{0:T(128)S(1)}, s32[2]{0:T(128)}, u32[]{:S(2)}) copy-start(s32[2]{0:T(128)} %param.24) | copy-start | bytes 28
  36.0 7.1 copy-start.6
  48.5 7.1 copy-start.23
  55.6 479.2 %all-reduce.8.cloned.1.call-start = ((), (), s32[]{:S(2)}) async-start(), calls=%async_computation.8 | async-start | bytes 12582912 | tf_op jit(solution)/shard_map/psum | solution.py:145
  288.2 18.5 %copy-start.9 = (bf16[2048,768]{1,0:T(8,128)(2,1)}, bf16[2048,768]{1,0:T(8,128)(2,1)S(1)}, u32[]{:S(2)}) copy-start(bf16[2048,768]{1,0:T(8,128)(2,1)S(1)} %fusion.103) | copy-start | bytes 9437188
  288.2 20.2 %copy-start.38 = (bf16[768,768]{1,0:T(8,128)(2,1)S(1)}, bf16[768,768]{1,0:T(8,128)(2,1)}, u32[]{:S(2)}) copy-start(bf16[768,768]{1,0:T(8,128)(2,1)} %param.35) | copy-start | bytes 3538948
  312.9 477.7 %all-reduce.10.cloned.1.call-start = ((), (), s32[]{:S(2)}) async-start(), calls=%async_computation.9 | async-start | bytes 12582912 | tf_op jit(solution)/shard_map/psum | solution.py:175
  542.4 10.5 slice-start.1
  552.9 9.5 copy-start.4
  568.7 221.9 %copy-start.22 = (f32[768]{0:T(1024)S(1)}, f32[768]{0:T(1024)}, u32[]{:S(2)}) copy-start(f32[768]{0:T(1024)} %get-tuple-element.469) | copy-start | bytes 9220
  568.7 339.6 %reduce-scatter.31.cloned.1.call-start = ((), (), s32[]{:S(2)}) async-start(), calls=%async_computation.17 | async-start | bytes 442368
  570.3 339.4 %reduce-scatter.29.cloned.1.call-start = ((), (), s32[]{:S(2)}) async-start(), calls=%async_computation.16 | async-start | bytes 442368
  571.4 355.0 %reduce-scatter.27.cloned.1.call-start = ((), (), s32[]{:S(2)}) async-start(), calls=%async_computation.15 | async-start | bytes 442368
  798.8 7.4 copy-start.12
  803.5 8.3 copy-start.41
  837.7 6.6 copy-start.11
  837.7 6.6 copy-start.24
  837.7 6.6 copy-start.43
  838.7 99.5 %reduce-scatter.25.cloned.1.call-start = ((), (), s32[]{:S(2)}) async-start(), calls=%async_computation.14 | async-start | bytes 884736
  843.9 137.8 %reduce-scatter.23.cloned.1.call-start = ((), (), s32[]{:S(2)}) async-start(), calls=%async_computation.13 | async-start | bytes 2211840
  853.8 12.5 copy-start.13
  871.4 9.0 copy-start.14
  871.4 9.0 copy-start.15
  880.4 326.6 %all-reduce.12.cloned.1.call-start = ((), (), s32[]{:S(2)}) async-start(), calls=%async_computation.10 | async-start | bytes 12582912 | tf_op jit(solution)/shard_map/psum | solution.py:226
  886.5 365.6 %reduce-scatter.21.cloned.1.call-start = ((), (), s32[]{:S(2)}) async-start(), calls=%async_computation.12 | async-start | bytes 2654208 | tf_op jit(solution)/shard_map/reduce_scatter | solution.py:171
  894.5 7.3 copy-start.44
  894.5 403.9 %reduce-scatter.19.cloned.1.call-start = ((), (), s32[]{:S(2)}) async-start(), calls=%async_computation.11 | async-start | bytes 2654208 | tf_op jit(solution)/shard_map/reduce_scatter | solution.py:170
  1207.0 91.4 %copy-start.1 = (bf16[768,768]{1,0:T(8,128)(2,1)S(1)}, bf16[768,768]{1,0:T(8,128)(2,1)}, u32[]{:S(2)}) copy-start(bf16[768,768]{1,0:T(8,128)(2,1)} %param.33) | copy-start | bytes 3538948
  (37 other events, 80.8 us)
Sparse Core Ops, SparseCore 0:
  55.7 225.5 all-reduce.5
  313.0 221.7 all-reduce.7
  568.9 221.7 all-reduce.9
  793.5 32.7 reduce-scatter.30
  829.3 33.8 reduce-scatter.28
  866.1 33.8 reduce-scatter.26
  903.2 34.9 reduce-scatter.24
  941.6 40.1 reduce-scatter.22
  984.1 222.8 all-reduce.11
  1210.8 41.2 reduce-scatter.20
  1256.0 42.3 reduce-scatter.18
where the time goes:
time: 1310 us
  waiting for transfers between devices  1020 us (78%)
  matrix products  109 us (8%)
  local copies, waits for them, and re-layouts  84.2 us (6%)
  other arithmetic  59.6 us (5%)
  between operations  15.9 us (1%)
  blocking collectives  13.6 us (1%)
    psum x1, waiting for transfers between devices, on_device(): grad_tokens = grad_first + lax.psum(token_part, 'tensor')  223 us
    psum x1, waiting for transfers between devices, on_device(): attn_total = lax.psum(attn_part, 'tensor')  223 us
    psum x1, waiting for transfers between devices, on_device(): ffn_total = lax.psum(ffn_part, 'tensor')  222 us
    psum x1, waiting for transfers between devices, on_device(): grad_first_out = grad_second + lax.psum(input_part, 'tensor')  219 us
    unnamed x16, waiting for transfers between devices  50.9 us
    reduce_scatter x1, waiting for transfers between devices, on_device(): lax.psum_scatter(grad_up, 'dp', scatter_dimension=0, tiled=True)  46.3 us
    reduce_scatter x1, waiting for transfers between devices, on_device(): lax.psum_scatter(grad_down, 'dp', scatter_dimension=1, tiled=True)  35.8 us
    unnamed x111, local copies, waits for them, and re-layouts  27.9 us
  transfers between devices with their start and end apart: 11, of which 8 were waited for; matrix products, arithmetic and copies ran while one was open for 10% of the time, Pallas kernels for 0%

commit v1 on v0

--- a/solution.py
+++ b/solution.py
@@ -92,6 +92,12 @@
     short_cotangent,
     long_cotangent,
 ):
+
+    def finish_orders_over_axis(piece_in, axis_key="tensor"):
+        n_now = lax.all_gather(piece_in, axis_key)
+        part_now = jnp.sum(n_now, 0)
+        return part_now
+
     short_pairs, short_slot, model_width = short_tokens.shape
     long_pairs, long_slot = (long_tokens.shape[0], long_tokens.shape[1])
     short_rows = short_pairs * short_slot
@@ -142,7 +148,7 @@
     )
     activated = gelu_exact(inner).astype(jnp.bfloat16)
     ffn_part = jnp.dot(activated, w_down, preferred_element_type=jnp.float32)
-    ffn_total = lax.psum(ffn_part, "tensor")
+    ffn_total = finish_orders_over_axis(ffn_part)
     normed_two, factor_two = normalize(first_out + ffn_total + bias_float[1])
     encoded = (normed_two * gain_rows[1] + shift_rows[1]).astype(jnp.bfloat16)
     upstream = jnp.concatenate(

time: 1310 us -> 1520 us (1.16)
  waiting for transfers between devices: 1020 us -> 1230 us
    all_gather x0 -> x1, waiting for transfers between devices: none -> 424 us  [finish_orders_over_axis(): n_now = lax.all_gather(piece_in, axis_key)]
    psum x1 -> x0, waiting for transfers between devices: 222 us -> none  [on_device(): ffn_total = lax.psum(ffn_part, 'tensor')]
  transfers between devices with their start and end apart: 11 -> 11, of which waited for: 8 -> 8; matrix products, arithmetic and copies ran while one was open for 10% -> 8% of each run, Pallas kernels for 0% -> 0%
where the time goes in v1:
time: 1520 us; the launch traced here: 1510 us
  waiting for transfers between devices  1230 us (81%)
  matrix products  106 us (7%)
  local copies, waits for them, and re-layouts  75.9 us (5%)
  other arithmetic  68.6 us (5%)
  between operations  16.1 us (1%)
    all_gather x1, waiting for transfers between devices, finish_orders_over_axis(): n_now = lax.all_gather(piece_in, axis_key)  424 us
    psum x1, waiting for transfers between devices, on_device(): attn_total = lax.psum(attn_part, 'tensor')  225 us
    psum x1, waiting for transfers between devices, on_device(): grad_tokens = grad_first + lax.psum(token_part, 'tensor')  223 us
    psum x1, waiting for transfers between devices, on_device(): grad_first_out = grad_second + lax.psum(input_part, 'tensor')  219 us
    unnamed x16, waiting for transfers between devices  57 us
    reduce_scatter x1, waiting for transfers between devices, on_device(): lax.psum_scatter(grad_down, 'dp', scatter_dimension=1, tiled=True)  46.3 us
    reduce_scatter x1, waiting for transfers between devices, on_device(): lax.psum_scatter(grad_up, 'dp', scatter_dimension=0, tiled=True)  35.8 us
  transfers between devices with their start and end apart: 11, of which 8 were waited for; matrix products, arithmetic and copies ran while one was open for 8% of the time, Pallas kernels for 0%

profile of v1, /device:TPU:0, one launch (start us, length us, event | category | flops | bytes accessed | tf_op | source)
XLA Modules:
  0.0 1512.4 jit_solution(10701474615497624901)
XLA Ops:
  8.3 4.1 fusion.122
  14.4 4.0 while.52
  28.3 16.0 %while.53 = (s32[]{:T(128)}, bf16[3,512,3,64]{1,3,2,0:T(8,128)(2,1)}, f32[3,3,512]{2,1,0:T(4,128)S(1)}, bf16[3,512,3,64]{1,3,2,0:T(8,128)(2,1)}, s32[3]{0:T(128)...) while((s32[]{:T(128)}, bf16[3,512,3,64]{1,3,2,0:T(8,128)(2,1)}, ...), condition=%wide.region_7.8_spmd, body=%wide.region_4.7_spmd.sunk | while | flops 210861056 | bytes 10283121 | solution.py:135
  50.6 225.0 %all-reduce.5.cloned.1.call-done = f32[2048,768]{1,0:T(8,128)} async-done(((f32[2048,768]{1,0:T(8,128)}), f32[2048,768]{1,0:T(8,128)}) %all-reduce.5.cloned.1.call-update) | async-done | bytes 6291472 | tf_op jit(solution)/shard_map/psum | solution.py:142
  275.6 4.2 fusion.130
  282.5 18.4 %multiply_convert_fusion.2 = (bf16[2048,768]{1,0:T(8,128)(2,1)S(1)}, f32[2048,768]{1,0:T(8,128)}, f32[2048,768]{1,0:T(8,128)}) fusion(f32[768]{0:T(1024)S(1)} %convert_reduce_fusion.3, bf16[2048,768]{1,0:T(8,128)(2,1)S(1)} %fusion.103, bf16[768,768]{1,0:T(8,128)(2,1)S(1)} %copy-done), kind=kOutput, calls=%fused_computation.132 | convolution fusion | flops 2519728128 | bytes 20057088 | tf_op jit(solution)/shard_map/dot_general | solution.py:146
  302.6 4.4 fusion.138
  307.2 424.0 %all-gather.3.cloned.1.call-done = f32[8192,768]{1,0:T(8,128)} async-done(((f32[2048,768]{1,0:T(8,128)}), f32[8192,768]{1,0:T(8,128)}) %all-gather.3.cloned.1.call-update) | async-done | bytes 25165840 | tf_op jit(solution)/shard_map/all_gather | solution.py:97
  731.2 12.6 reduce_sum.191
  743.8 5.7 fusion.128
  755.4 5.3 fusion.126
  760.7 9.0 convert_reduce_fusion.1
  771.3 4.5 fusion.139
  778.2 218.8 %all-reduce.7.cloned.1.call-done = f32[2048,768]{1,0:T(8,128)} async-done(((f32[2048,768]{1,0:T(8,128)}), f32[2048,768]{1,0:T(8,128)}) %all-reduce.7.cloned.1.call-update) | async-done | bytes 6291472 | tf_op jit(solution)/shard_map/psum | solution.py:181
  997.0 8.1 multiply_reduce_fusion.2
  1005.2 4.7 fusion.125
  1016.3 22.0 %while.55 = (s32[]{:T(128)}, bf16[3,512,3,64]{1,3,2,0:T(8,128)(2,1)}, bf16[3,512,3,64]{1,3,2,0:T(8,128)(2,1)}, bf16[3,512,3,64]{1,3,2,0:T(8,128)(2,1)}, bf16[3,5...) while((s32[]{:T(128)}, ...), condition=%wide.region_24.25_spmd, body=%wide.region_22.24_spmd.sunk | while | flops 510589952 | bytes 40343856 | solution.py:203
  1039.5 5.0 fusion.119
  1045.0 9.6 while.54
  1068.8 4.9 fusion.116
  1073.8 4.4 copy.129
  1078.2 4.7 reshape.243
  1083.0 4.8 convolution_bitcast_fusion.1
  1087.8 7.0 fusion.140
  1095.2 7.9 fusion.110
  1113.4 13.3 all-reduce
  1130.4 14.8 reduce-scatter.25.cloned.1.call-done
  1146.8 42.0 %reduce-scatter.23.cloned.1.call-done = f32[96,576]{1,0:T(8,128)} async-done(((f32[768,576]{1,0:T(8,128)}), f32[96,576]{1,0:T(8,128)}) %reduce-scatter.23.cloned.1.call-update) | async-done | bytes 221200
  1190.7 223.4 %all-reduce.9.cloned.1.call-done = f32[2048,768]{1,0:T(8,128)} async-done(((f32[2048,768]{1,0:T(8,128)}), f32[2048,768]{1,0:T(8,128)}) %all-reduce.9.cloned.1.call-update) | async-done | bytes 6291472 | tf_op jit(solution)/shard_map/psum | solution.py:232
  1414.0 5.5 add.173
  1423.3 35.8 %reduce-scatter.19.cloned.1.call-done = f32[96,768]{1,0:T(8,128)} async-done(((f32[768,768]{1,0:T(8,128)}), f32[96,768]{1,0:T(8,128)}) %reduce-scatter.19.cloned.1.call-update) | async-done | bytes 294928 | tf_op jit(solution)/shard_map/reduce_scatter | solution.py:176
  1459.1 46.3 %reduce-scatter.21.cloned.1.call-done = f32[768,96]{0,1:T(8,128)} async-done(((f32[768,768]{0,1:T(8,128)}), f32[768,96]{0,1:T(8,128)}) %reduce-scatter.21.cloned.1.call-update) | async-done | bytes 294928 | tf_op jit(solution)/shard_map/reduce_scatter | solution.py:177
  (339 shorter events, 127.3 us)
Async XLA Ops:
  7.2 275.3 %copy-start = (bf16[768,768]{1,0:T(8,128)(2,1)S(1)}, bf16[768,768]{1,0:T(8,128)(2,1)}, u32[]{:S(2)}) copy-start(bf16[768,768]{1,0:T(8,128)(2,1)} %param.33) | copy-start | bytes 3538948
  7.2 268.4 %all-reduce.5.cloned.1.call-start = ((), (), s32[]{:S(2)}) async-start(), calls=%async_computation.7 | async-start | bytes 12582912 | tf_op jit(solution)/shard_map/psum | solution.py:142
  18.5 9.8 copy-start.43
  28.3 17.8 %copy-start.21 = (bf16[192,768]{1,0:T(8,128)(2,1)S(1)}, bf16[192,768]{1,0:T(8,128)(2,1)}, u32[]{:S(2)}) copy-start(bf16[192,768]{1,0:T(8,128)(2,1)} %param.29) | copy-start | bytes 884740
  49.9 681.3 %all-gather.3.cloned.1.call-start = ((), (), s32[]{:S(2)}) async-start(), calls=%async_computation.12 | async-start | bytes 31457280 | tf_op jit(solution)/shard_map/all_gather | solution.py:97
  282.5 18.4 %copy-start.14 = (bf16[2048,768]{1,0:T(8,128)(2,1)}, bf16[2048,768]{1,0:T(8,128)(2,1)S(1)}, u32[]{:S(2)}) copy-start(bf16[2048,768]{1,0:T(8,128)(2,1)S(1)} %fusion.103) | copy-start | bytes 9437188
  282.5 20.0 %copy-start.40 = (bf16[768,768]{1,0:T(8,128)(2,1)S(1)}, bf16[768,768]{1,0:T(8,128)(2,1)}, u32[]{:S(2)}) copy-start(bf16[768,768]{1,0:T(8,128)(2,1)} %param.35) | copy-start | bytes 3538948
  307.0 690.0 %all-reduce.7.cloned.1.call-start = ((), (), s32[]{:S(2)}) async-start(), calls=%async_computation.8 | async-start | bytes 12582912 | tf_op jit(solution)/shard_map/psum | solution.py:181
  751.3 9.3 slice-start.1
  760.6 9.0 copy-start.4
  775.9 333.8 %reduce-scatter.31.cloned.1.call-start = ((), (), s32[]{:S(2)}) async-start(), calls=%async_computation.17 | async-start | bytes 442368
  776.9 334.1 %reduce-scatter.29.cloned.1.call-start = ((), (), s32[]{:S(2)}) async-start(), calls=%async_computation.16 | async-start | bytes 442368
  778.0 349.4 %reduce-scatter.27.cloned.1.call-start = ((), (), s32[]{:S(2)}) async-start(), calls=%async_computation.15 | async-start | bytes 442368
  1016.3 23.2 %copy-start.11 = (bf16[2048,192]{0,1:T(8,128)(2,1)S(1)}, bf16[2048,192]{0,1:T(8,128)(2,1)}, u32[]{:S(2)}) copy-start(bf16[2048,192]{0,1:T(8,128)(2,1)} %copy-done.10) | copy-start | bytes 2359300
  1038.3 6.6 copy-start.16
  1038.4 6.6 copy-start.35
  1038.4 6.6 copy-start.45
  1039.4 105.7 %reduce-scatter.25.cloned.1.call-start = ((), (), s32[]{:S(2)}) async-start(), calls=%async_computation.14 | async-start | bytes 884736
  1044.7 144.1 %reduce-scatter.23.cloned.1.call-start = ((), (), s32[]{:S(2)}) async-start(), calls=%async_computation.13 | async-start | bytes 2211840
  1054.6 14.2 copy-start.17
  1073.7 9.2 copy-start.18
  1073.7 9.2 copy-start.19
  1073.7 9.2 copy-start.20
  1073.7 9.2 copy-start.23
  1073.7 9.2 copy-start.25
  1073.7 9.2 copy-start.27
  1073.8 9.2 copy-start.42
  1082.9 331.2 %all-reduce.9.cloned.1.call-start = ((), (), s32[]{:S(2)}) async-start(), calls=%async_computation.9 | async-start | bytes 12582912 | tf_op jit(solution)/shard_map/psum | solution.py:232
  1087.8 371.3 %reduce-scatter.19.cloned.1.call-start = ((), (), s32[]{:S(2)}) async-start(), calls=%async_computation.10 | async-start | bytes 2654208 | tf_op jit(solution)/shard_map/reduce_scatter | solution.py:176
  1094.9 8.3 copy-start.46
  1094.9 410.5 %reduce-scatter.21.cloned.1.call-start = ((), (), s32[]{:S(2)}) async-start(), calls=%async_computation.11 | async-start | bytes 2654208 | tf_op jit(solution)/shard_map/reduce_scatter | solution.py:177
  1414.0 91.4 %copy-start.1 = (bf16[768,768]{1,0:T(8,128)(2,1)S(1)}, bf16[768,768]{1,0:T(8,128)(2,1)}, u32[]{:S(2)}) copy-start(bf16[768,768]{1,0:T(8,128)(2,1)} %param.33) | copy-start | bytes 3538948
  (43 other events, 103.0 us)
Sparse Core Ops, SparseCore 0:
  50.0 225.5 all-reduce.4
  307.1 424.0 all-gather.2
  776.0 221.0 all-reduce.6
  999.9 32.7 reduce-scatter.30
  1035.7 33.9 reduce-scatter.28
  1072.6 33.8 reduce-scatter.26
  1110.2 34.9 reduce-scatter.24
  1148.6 40.1 reduce-scatter.22
  1191.2 222.8 all-reduce.8
  1417.8 41.2 reduce-scatter.18
  1463.0 42.3 reduce-scatter.20
